TPU v7x, 512 devices: a whole 4x8x8 slice. The times are simulated.
512 devices in a mesh: seq: 32 (over x, y), req: 16 (over z, core).
Axes of the slice: x: 4, y: 8, z: 8, core: 2. Of those that a mesh axis runs over, the one named last changes fastest.
Arguments:
- x_in: bfloat16 [96, 4, 1536], P('req'), may hold values from -6 to 6
- attn_gain: float32 [1536], replicated, may hold values from 0.25 to 1.75
- moe_gain: float32 [1536], replicated, may hold values from 0.25 to 1.75
- w_qkv: bfloat16 [1536, 2560], P(None, 'seq'), may hold values from -0.15625 to 0.15625
- w_o: bfloat16 [1536, 1536], P(None, 'seq'), may hold values from -0.3125 to 0.3125
- cache_k: bfloat16 [96, 4096, 512], P('req', 'seq'), may hold values from -1024 to 1024
- cache_v: bfloat16 [96, 4096, 512], P('req', 'seq'), may hold values from -6 to 6
- page_map: int32 [96, 256], P('req', 'seq'), may hold values from 0 to 255, as said below
- lengths: int32 [96], P('req'), may hold values from 2 to 4096, as said below
- routes: int32 [96, 4, 8], P('req'), may hold values from 0 to 31, all different within a row; in each aligned block of 24 rows (0 to 23, 24 to 47, ..., all dimensions but the last counted through in order) at most 12 rows name the same one
- route_weights: float32 [96, 4, 8], P('req'), may hold values from 0.1 to 1
- w_gate_up: bfloat16 [32, 1536, 1024], P('seq', 'req'), may hold values from -0.15625 to 0.15625
- w_down: bfloat16 [32, 512, 1536], P('seq', None, 'req'), may hold values from -0.375 to 0.375
Outputs:
- layer_out: bfloat16 [96, 4, 1536], P('req', None, 'seq')
Inputs may be any that keep to these rules, and one draw needn't show every extreme that they name: `lengths`: every index of req holds one request with exactly 4096 cached positions. `page_map`: each row is a permutation of the request's 256 logical pages. `routes`: A token names 8 different experts. Among the 24 tokens of one index of req no expert is named more than 12 times.
All inputs are finite; a program needn't handle non-finite values.
Results may differ from a plain program's by a relative error of at most 0.01.
Values may be sent and summed in bfloat16 or wider, within the bound.
A program may use at most 64 MiB of HBM per device.

v0:
```python
import math
import jax
import jax.numpy as jnp
from jax import lax
from jax.sharding import PartitionSpec as P

D = 1536
HEADS = 24
KVH = 8
HD = 64
FFE = 512
TOP = 8
NSTEP = 4
PAGE = 16
ATT = 1536
KVD = 512
GROUP = 3
CAP = 12
EPS = 1e-05
NEG = -1e30


def normalize(values, gain):
    power = jnp.mean(values * values, axis=-1, keepdims=True)
    return values * lax.rsqrt(power + EPS) * gain


def rotate(values, position):
    half = values.shape[-1] // 2
    rates = jnp.exp(
        jnp.arange(half, dtype=jnp.float32) * (-2.0 * math.log(10000.0) / values.shape[-1])
    )
    angle = position[..., None, None] * rates
    cosine = jnp.cos(angle)
    sine = jnp.sin(angle)
    first_half = values[..., :half]
    second_half = values[..., half:]
    return jnp.concatenate(
        [first_half * cosine - second_half * sine, second_half * cosine + first_half * sine],
        axis=-1,
    )


def gather_columns(part, axis_name):
    count = lax.axis_size(axis_name)
    copies = jnp.broadcast_to(part[None], (count,) + part.shape)
    pieces = lax.all_to_all(copies, axis_name, split_axis=0, concat_axis=0, tiled=True)
    rows, width = part.shape
    return jnp.moveaxis(pieces, 0, 1).reshape(rows, count * width)


def sum_scatter_columns(value, axis_name):
    count = lax.axis_size(axis_name)
    rows, width = value.shape
    chunks = jnp.moveaxis(value.reshape(rows, count, width // count), 1, 0)
    pieces = lax.all_to_all(chunks, axis_name, split_axis=0, concat_axis=0, tiled=True)
    return jnp.sum(pieces, axis=0)


def local(
    x_in,
    attn_gain,
    moe_gain,
    w_qkv,
    w_o,
    cache_k,
    cache_v,
    page_map,
    lengths,
    routes,
    route_weights,
    w_gate_up,
    w_down,
):
    pieces = 4
    expert_in = jnp.concatenate(
        [
            lax.all_gather(part, "req", axis=0, tiled=True)
            for part in jnp.split(w_gate_up[0], pieces, axis=1)
        ],
        axis=1,
    )
    expert_out = jnp.concatenate(
        [
            lax.all_gather(part, "req", axis=1, tiled=True)
            for part in jnp.split(w_down[0], pieces // 2, axis=0)
        ],
        axis=0,
    )
    seq_count = lax.axis_size("seq")
    me = lax.axis_index("seq")
    local_requests = x_in.shape[0]
    row_count = local_requests * NSTEP
    inputs = x_in.astype(jnp.float32).reshape(row_count, D)
    normed = normalize(inputs, attn_gain).astype(jnp.bfloat16)
    projected = gather_columns(jnp.dot(normed, w_qkv, preferred_element_type=jnp.float32), "seq")
    queries = projected[:, :ATT].reshape(local_requests, NSTEP, HEADS, HD)
    keys_new = projected[:, ATT : ATT + KVD].reshape(local_requests, NSTEP, KVH, HD)
    values_new = (
        projected[:, ATT + KVD :].reshape(local_requests, NSTEP, KVH, HD).astype(jnp.bfloat16)
    )
    position = (lengths[:, None] + jnp.arange(NSTEP, dtype=jnp.int32)[None, :]).astype(jnp.float32)
    queries = (
        rotate(queries, position)
        .astype(jnp.bfloat16)
        .reshape(local_requests, NSTEP, KVH, GROUP, HD)
    )
    keys_new = rotate(keys_new, position).astype(jnp.bfloat16)
    scale = HD ** (-0.5)
    slot_count = cache_k.shape[1]
    cached_keys = cache_k.reshape(local_requests, slot_count, KVH, HD)
    cached_values = cache_v.reshape(local_requests, slot_count, KVH, HD)
    slot_position = (
        page_map[:, :, None] * PAGE + jnp.arange(PAGE, dtype=jnp.int32)[None, None, :]
    ).reshape(local_requests, slot_count)
    live = (slot_position < lengths[:, None])[:, None, None, None, :]
    scores = (
        jnp.einsum("rskgd,rtkd->rskgt", queries, cached_keys, preferred_element_type=jnp.float32)
        * scale
    )
    scores = jnp.where(live, scores, NEG)
    local_top = jnp.max(scores, axis=-1)
    exp_scores = jnp.where(live, jnp.exp(scores - local_top[..., None]), 0.0)
    local_total = jnp.sum(exp_scores, axis=-1).reshape(row_count, HEADS)
    local_sums = jnp.einsum(
        "rskgt,rtkd->rskgd",
        exp_scores.astype(jnp.bfloat16),
        cached_values,
        preferred_element_type=jnp.float32,
    ).reshape(row_count, ATT)
    local_top = local_top.reshape(row_count, HEADS)
    width = ATT // seq_count
    sum_chunks = jnp.moveaxis(local_sums.reshape(row_count, seq_count, width), 1, 0)
    extras = jnp.broadcast_to(
        jnp.concatenate([local_total, local_top], axis=1)[None], (seq_count, row_count, 2 * HEADS)
    )
    outgoing = jnp.concatenate([sum_chunks, extras], axis=2)
    arrived = lax.all_to_all(outgoing, "seq", split_axis=0, concat_axis=0, tiled=True)
    part_sums = arrived[:, :, :width]
    part_totals = arrived[:, :, width : width + HEADS]
    part_tops = arrived[:, :, width + HEADS :]
    causal = (
        jnp.arange(NSTEP, dtype=jnp.int32)[:, None] >= jnp.arange(NSTEP, dtype=jnp.int32)[None, :]
    )[None, :, None, None, :]
    fresh = (
        jnp.einsum("rskgd,rukd->rskgu", queries, keys_new, preferred_element_type=jnp.float32)
        * scale
    )
    fresh = jnp.where(causal, fresh, NEG).reshape(row_count, HEADS, NSTEP)
    cache_top = jnp.max(part_tops, axis=0)
    highest = jnp.maximum(cache_top, jnp.max(fresh, axis=-1))
    factors = jnp.exp(part_tops - highest[None])
    fresh_exp = jnp.exp(fresh - highest[:, :, None])
    denominator = jnp.sum(part_totals * factors, axis=0) + jnp.sum(fresh_exp, axis=-1)
    fresh_probs = fresh_exp.reshape(local_requests, NSTEP, KVH, GROUP, NSTEP).astype(jnp.bfloat16)
    fresh_sums = jnp.einsum(
        "rskgu,rukd->rskgd", fresh_probs, values_new, preferred_element_type=jnp.float32
    ).reshape(row_count, ATT)
    start = me * width
    head_of = (start + jnp.arange(width, dtype=jnp.int32)) // HD
    chunk_factors = jnp.take(factors, head_of, axis=2)
    numerator = jnp.sum(part_sums * chunk_factors, axis=0) + lax.dynamic_slice_in_dim(
        fresh_sums, start, width, 1
    )
    chunk_denominator = jnp.take(denominator, head_of, axis=1)
    attended_part = (numerator / chunk_denominator).astype(jnp.bfloat16)
    attended = gather_columns(attended_part, "seq")
    attn_mixed = gather_columns(jnp.dot(attended, w_o, preferred_element_type=jnp.float32), "seq")
    resid = inputs + attn_mixed
    mixed_in = normalize(resid, moe_gain).astype(jnp.bfloat16)
    expert = me
    chosen = routes.reshape(row_count, TOP)
    gates = route_weights.reshape(row_count, TOP)
    route_scale = jnp.sum(jnp.where(chosen == expert, gates, 0.0), axis=-1)
    gate_up = jnp.dot(mixed_in, expert_in, preferred_element_type=jnp.float32)
    hidden = (jax.nn.silu(gate_up[:, :FFE]) * gate_up[:, FFE:]).astype(jnp.bfloat16)
    produced = jnp.dot(hidden, expert_out, preferred_element_type=jnp.float32)
    own_share = sum_scatter_columns(route_scale[:, None] * produced, "seq")
    share_width = own_share.shape[1]
    resid_share = lax.dynamic_slice_in_dim(resid, me * share_width, share_width, 1)
    return (
        (resid_share + own_share).astype(jnp.bfloat16).reshape(local_requests, NSTEP, share_width)
    )


def solution(mesh):
    in_specs = (
        P("req", None, None),
        P(),
        P(),
        P(None, "seq"),
        P(None, "seq"),
        P("req", "seq", None),
        P("req", "seq", None),
        P("req", "seq"),
        P("req"),
        P("req", None, None),
        P("req", None, None),
        P("seq", "req", None),
        P("seq", None, "req"),
    )
    out_specs = P("req", None, "seq")
    return jax.shard_map(local, mesh=mesh, in_specs=in_specs, out_specs=out_specs, check_vma=False)
```

profile of v0, /device:TPU:8, one launch (start us, length us, event | category | flops | bytes accessed | tf_op | source)
XLA Modules:
  0.0 217.1 jit_solution(889715388834273330)
XLA Ops:
  0.0 0.9 reshape.269
  0.9 1.0 multiply_reduce_fusion.2
  2.1 1.0 fusion.26
  3.1 0.8 broadcast_in_dim.66
  3.9 10.2 %all-to-all-start = ((f32[32,24,80]{2,1,0:T(8,128)}), f32[32,24,80]{2,1,0:T(8,128)S(1)}, u32[]{:S(2)}, u32[]{:S(2)}) async-start(f32[32,24,80]{2,1,0:T(8,128)} %broadcast_in_dim.66), calls=%async_computation | async-start | bytes 786432 | tf_op jit(solution)/shard_map/all_to_all | solution.py:47
  14.4 0.4 copy.66
  14.8 0.8 copy-done.4
  15.5 1.2 copy.67
  16.8 25.3 %all_gather.18 = bf16[1536,256]{1,0:T(8,128)(2,1)S(1)} all-gather(bf16[96,256]{1,0:T(8,128)(2,1)S(1)} %get-tuple-element.14), channel_id=1, replica_groups=mesh['seq'=32,'req'=16] {'req'}, dimensions={0}, use_global_device_ids=true | all-gather | bytes 835584 | tf_op jit(solution)/shard_map/all_gather | solution.py:78
  42.1 18.1 %all_gather.19 = bf16[1536,256]{1,0:T(8,128)(2,1)} all-gather(bf16[96,256]{1,0:T(8,128)(2,1)S(1)} %get-tuple-element.17), channel_id=1, replica_groups=mesh['seq'=32,'req'=16] {'req'}, dimensions={0}, use_global_device_ids=true | all-gather | bytes 835584 | tf_op jit(solution)/shard_map/all_gather | solution.py:78
  60.2 19.3 %all_gather.20 = bf16[1536,256]{1,0:T(8,128)(2,1)} all-gather(bf16[96,256]{1,0:T(8,128)(2,1)S(1)} %get-tuple-element.16), channel_id=1, replica_groups=mesh['seq'=32,'req'=16] {'req'}, dimensions={0}, use_global_device_ids=true | all-gather | bytes 835584 | tf_op jit(solution)/shard_map/all_gather | solution.py:78
  79.8 18.0 %all_gather.21 = bf16[1536,256]{1,0:T(8,128)(2,1)} all-gather(bf16[96,256]{1,0:T(8,128)(2,1)S(1)} %get-tuple-element.15), channel_id=1, replica_groups=mesh['seq'=32,'req'=16] {'req'}, dimensions={0}, use_global_device_ids=true | all-gather | bytes 835584 | tf_op jit(solution)/shard_map/all_gather | solution.py:78
  98.5 0.4 copy-done.1
  99.0 0.5 fusion.47
  99.5 0.4 copy.70
  99.9 0.5 fusion.18
  100.4 0.4 copy.69
  101.0 0.6 convolution_bitcast_fusion
  101.7 0.3 reshape_reshape.3
  102.4 0.9 pad_maximum_fusion
  103.3 9.9 %all-to-all-start.1 = ((f32[32,24,96]{2,1,0:T(8,128)}), f32[32,24,96]{2,1,0:T(8,128)S(1)}, u32[]{:S(2)}, u32[]{:S(2)}) async-start(f32[32,24,96]{2,1,0:T(8,128)} %pad_maximum_fusion), calls=%async_computation.1 | async-start | bytes 786432 | tf_op jit(solution)/shard_map/all_to_all | solution.py:138
  113.6 1.1 fusion.48
  114.9 13.8 %all-to-all-done.1 = f32[32,24,96]{2,1,0:T(8,128)S(1)} async-done(((f32[32,24,96]{2,1,0:T(8,128)}), f32[32,24,96]{2,1,0:T(8,128)S(1)}, u32[]{:S(2)}, u32[]{:S(2)}) %all-to-all-start.1) | async-done | bytes 294944 | tf_op jit(solution)/shard_map/all_to_all | solution.py:138
  128.6 0.3 slice_reduce_fusion
  129.1 0.3 fusion.16
  129.4 0.4 convolution_bitcast_fusion.1
  129.9 0.3 reshape.277
  130.7 0.3 copy.105
  131.1 0.3 multiply_reduce_fusion
  131.4 0.6 gather_fusion
  132.1 0.6 gather_fusion.1
  132.6 0.3 fusion.15
  133.2 0.9 reshape.308
  134.1 4.8 %all-to-all-start.2 = ((bf16[32,2,576]{2,1,0:T(2,128)(2,1)}), bf16[32,2,576]{2,1,0:T(2,128)(2,1)S(1)}, u32[]{:S(2)}, u32[]{:S(2)}) async-start(bf16[32,2,576]{2,1,0:T(2,128)(2,1)} %reshape.308), calls=%async_computation.2 | async-start | bytes 163840 | tf_op jit(solution)/shard_map/all_to_all | solution.py:47
  138.9 19.5 %all-gather = bf16[1,256,1536]{1,2,0:T(8,128)(2,1)} all-gather(bf16[1,256,96]{1,2,0:T(8,128)(2,1)S(1)} %get-tuple-element.20), channel_id=2, replica_groups=mesh['seq'=32,'req'=16] {'req'}, dimensions={2}, use_global_device_ids=true | all-gather | bytes 835584 | tf_op jit(solution)/shard_map/all_gather | solution.py:85
  159.3 1.0 reshape.310
  160.3 9.8 %all-to-all-start.3 = ((f32[32,1,1152]{2,1,0:T(1,128)}), f32[32,1,1152]{2,1,0:T(1,128)S(1)}, u32[]{:S(2)}, u32[]{:S(2)}) async-start(f32[32,1,1152]{2,1,0:T(1,128)} %reshape.310), calls=%async_computation.3 | async-start | bytes 294912 | tf_op jit(solution)/shard_map/all_to_all | solution.py:47
  170.1 18.0 %all-gather.1 = bf16[1,256,1536]{1,2,0:T(8,128)(2,1)} all-gather(bf16[1,256,96]{1,2,0:T(8,128)(2,1)S(1)} %get-tuple-element.21), channel_id=3, replica_groups=mesh['seq'=32,'req'=16] {'req'}, dimensions={2}, use_global_device_ids=true | all-gather | bytes 835584 | tf_op jit(solution)/shard_map/all_gather | solution.py:85
  188.1 0.5 broadcast.243
  188.6 1.0 reduce.5
  190.1 0.3 reshape.280
  190.4 0.4 copy-done.9
  191.1 2.6 %fusion = f32[24,1024]{1,0:T(8,128)S(1)} fusion(bf16[1536,256]{1,0:T(8,128)(2,1)} %all_gather.21, bf16[1536,256]{1,0:T(8,128)(2,1)} %all_gather.20, bf16[1536,256]{1,0:T(8,128)(2,1)S(1)} %copy-done.5, bf16[1536,256]{1,0:T(8,128)(2,1)S(1)} %all_gather.18, f32[24,1536]{1,0:T(8,128)S(1)} %add.165, f32[1536]{0:T(1024)S(1)} %copy-done.17, f32[24]{0:T(128)S(1)} %rsqrt.25), kind=kOutput, calls=%fused_computation.2 | convolution fusion | flops 88190976 | bytes 3397728 | tf_op jit(solution)/shard_map/dot_general | solution.py:175
  193.7 0.5 convolution_multiply_fusion
  194.6 0.4 reshape.312
  195.0 20.2 %all_to_all.25 = f32[32,1,1152]{2,1,0:T(1,128)S(1)} all-to-all(f32[32,1,1152]{2,1,0:T(1,128)S(1)} %reshape.312), channel_id=1, replica_groups=mesh['seq'=32,'req'=16] {'seq'}, dimensions={0} | all-to-all | bytes 294912 | tf_op jit(solution)/shard_map/all_to_all | solution.py:56
  215.2 1.0 reduce.6
  216.4 0.7 add_convert_fusion.2
  (108 shorter events, 6.1 us)
Async XLA Ops:
  0.0 2.0 copy-start
  2.0 12.0 %copy-start.16 = (s32[6]{0:T(128)S(1)}, s32[6]{0:T(128)}, u32[]{:S(2)}) copy-start(s32[6]{0:T(128)} %param.21) | copy-start | bytes 76
  2.0 12.1 %copy-start.15 = (s32[6,8]{1,0:T(8,128)S(1)}, s32[6,8]{1,0:T(8,128)}, u32[]{:S(2)}) copy-start(s32[6,8]{1,0:T(8,128)} %param.20) | copy-start | bytes 580
  2.1 12.3 %copy-start.3 = (bf16[6,128,512]{2,1,0:T(8,128)(2,1)S(1)}, bf16[6,128,512]{2,1,0:T(8,128)(2,1)}, u32[]{:S(2)}) copy-start(bf16[6,128,512]{2,1,0:T(8,128)(2,1)} %param.18) | copy-start | bytes 2359300
  3.9 94.0 %all-to-all-start = ((f32[32,24,80]{2,1,0:T(8,128)}), f32[32,24,80]{2,1,0:T(8,128)S(1)}, u32[]{:S(2)}, u32[]{:S(2)}) async-start(f32[32,24,80]{2,1,0:T(8,128)} %broadcast_in_dim.66), calls=%async_computation | async-start | bytes 786432 | tf_op jit(solution)/shard_map/all_to_all | solution.py:47
  14.4 1.1 copy-start.4
  15.5 1.2 copy-start.10
  42.1 37.5 %copy-start.12 = (bf16[1,512,96]{1,2,0:T(8,128)(2,1)S(1)}, bf16[1,512,96]{1,2,0:T(8,128)(2,1)}, u32[]{:S(2)}) copy-start(bf16[1,512,96]{1,2,0:T(8,128)(2,1)} %param.25) | copy-start | bytes 294916
  98.2 0.7 copy-start.1
  99.5 1.5 copy-start.6
  102.4 10.9 %slice-start = ((f32[24,2560]{1,0:T(8,128)}), f32[24,512]{1,0:T(8,128)S(1)}, s32[]{:S(2)}) async-start(f32[24,2560]{1,0:T(8,128)} %copy-done.1), calls=%async_computation.5 | async-start | bytes 98304 | tf_op jit(solution)/shard_map/slice | solution.py:98
  103.3 10.1 %copy-start.2 = (f32[24,2560]{1,0:T(8,128)S(1)}, f32[24,2560]{1,0:T(8,128)}, u32[]{:S(2)}) copy-start(f32[24,2560]{1,0:T(8,128)} %copy-done.1) | copy-start | bytes 737284
  103.3 25.4 %all-to-all-start.1 = ((f32[32,24,96]{2,1,0:T(8,128)}), f32[32,24,96]{2,1,0:T(8,128)S(1)}, u32[]{:S(2)}, u32[]{:S(2)}) async-start(f32[32,24,96]{2,1,0:T(8,128)} %pad_maximum_fusion), calls=%async_computation.1 | async-start | bytes 786432 | tf_op jit(solution)/shard_map/all_to_all | solution.py:138
  132.9 25.4 %copy-start.13 = (f32[6,4,8]{2,1,0:T(4,128)S(1)}, f32[6,4,8]{2,1,0:T(4,128)}, u32[]{:S(2)}) copy-start(f32[6,4,8]{2,1,0:T(4,128)} %param.23) | copy-start | bytes 2308
  133.0 25.4 %copy-start.14 = (s32[6,4,8]{2,1,0:T(4,128)S(1)}, s32[6,4,8]{2,1,0:T(4,128)}, u32[]{:S(2)}) copy-start(s32[6,4,8]{2,1,0:T(4,128)} %param.22) | copy-start | bytes 2308
  134.1 24.4 %all-to-all-start.2 = ((bf16[32,2,576]{2,1,0:T(2,128)(2,1)}), bf16[32,2,576]{2,1,0:T(2,128)(2,1)S(1)}, u32[]{:S(2)}, u32[]{:S(2)}) async-start(bf16[32,2,576]{2,1,0:T(2,128)(2,1)} %reshape.308), calls=%async_computation.2 | async-start | bytes 163840 | tf_op jit(solution)/shard_map/all_to_all | solution.py:47
  138.9 20.2 %copy-start.11 = (bf16[1536,48]{0,1:T(8,128)(2,1)S(1)}, bf16[1536,48]{0,1:T(8,128)(2,1)}, u32[]{:S(2)}) copy-start(bf16[1536,48]{0,1:T(8,128)(2,1)} %param.17) | copy-start | bytes 442372
  160.3 27.8 %all-to-all-start.3 = ((f32[32,1,1152]{2,1,0:T(1,128)}), f32[32,1,1152]{2,1,0:T(1,128)S(1)}, u32[]{:S(2)}, u32[]{:S(2)}) async-start(f32[32,1,1152]{2,1,0:T(1,128)} %reshape.310), calls=%async_computation.3 | async-start | bytes 294912 | tf_op jit(solution)/shard_map/all_to_all | solution.py:47
  189.9 0.9 copy-start.9
  189.9 1.2 copy-start.5
  189.9 1.2 copy-start.17
  191.1 2.6 %copy-start.7 = (bf16[1,256,1536]{1,2,0:T(8,128)(2,1)S(1)}, bf16[1,256,1536]{1,2,0:T(8,128)(2,1)}, u32[]{:S(2)}) copy-start(bf16[1,256,1536]{1,2,0:T(8,128)(2,1)} %all-gather) | copy-start | bytes 2359300
  191.1 2.6 %copy-start.8 = (bf16[1,256,1536]{1,2,0:T(8,128)(2,1)S(1)}, bf16[1,256,1536]{1,2,0:T(8,128)(2,1)}, u32[]{:S(2)}) copy-start(bf16[1,256,1536]{1,2,0:T(8,128)(2,1)} %all-gather.1) | copy-start | bytes 2359300
where the time goes:
time: 218 us; the launch traced here: 217 us
  blocking collectives  139 us (64%)
  starting transfers between devices  34.6 us (16%)
  local copies, waits for them, and re-layouts  15.5 us (7%)
  waiting for transfers between devices  13.8 us (6%)
  other arithmetic  7.28 us (3%)
  matrix products  6.84 us (3%)
    all_gather x4, blocking collectives, local(): lax.all_gather(part, 'req', axis=0, tiled=True)  80.8 us
    all_gather x2, blocking collectives, local(): lax.all_gather(part, 'req', axis=1, tiled=True)  37.5 us
    all_to_all x3, starting transfers between devices, gather_columns(): lax.all_to_all(copies, axis_name, split_axis=0, concat_axis=0, tiled=True)  24.7 us
    all_to_all x1, blocking collectives, sum_scatter_columns(): lax.all_to_all(chunks, axis_name, split_axis=0, concat_axis=0, tiled=True)  20.2 us
    all_to_all x1, waiting for transfers between devices, local(): lax.all_to_all(outgoing, 'seq', split_axis=0, concat_axis=0, tiled=True)  13.8 us
    all_to_all x1, starting transfers between devices, local(): lax.all_to_all(outgoing, 'seq', split_axis=0, concat_axis=0, tiled=True)  9.92 us
    unnamed x49, local copies, waits for them, and re-layouts  6.93 us
  transfers between devices with their start and end apart: 4, of which 1 were waited for; matrix products, arithmetic and copies ran while one was open for 2% of the time, Pallas kernels for 0%

commit v1 on v0

--- a/solution.py
+++ b/solution.py
@@ -18,6 +18,13 @@
 CAP = 12
 EPS = 1e-05
 NEG = -1e30
+
+
+def all_by_exchange(x, axis, dim):
+    size = lax.axis_size(axis)
+    blocks = jnp.stack([x for _ in range(size)])
+    blocks = lax.all_to_all(blocks, axis, split_axis=0, concat_axis=0)
+    return jnp.concatenate(blocks, axis=dim)
 
 
 def normalize(values, gain):
@@ -74,10 +81,7 @@
 ):
     pieces = 4
     expert_in = jnp.concatenate(
-        [
-            lax.all_gather(part, "req", axis=0, tiled=True)
-            for part in jnp.split(w_gate_up[0], pieces, axis=1)
-        ],
+        [all_by_exchange(part, "req", 0) for part in jnp.split(w_gate_up[0], pieces, axis=1)],
         axis=1,
     )
     expert_out = jnp.concatenate(

time: 218 us -> 257 us (1.18)
  waiting for transfers between devices: 13.8 us -> 53.3 us
  starting transfers between devices: 34.6 us -> 28 us
    all_gather x4 -> x0, blocking collectives: 80.8 us -> none  [local(): lax.all_gather(part, 'req', axis=0, tiled=True)]
    all_to_all x0 -> x3, blocking collectives: none -> 73.1 us  [the longest x2 58.3 us: all_by_exchange(): blocks = lax.all_to_all(blocks, axis, split_axis=0, concat_axis=0)]
    all_to_all x3 -> x2, waiting for transfers between devices: 0.01 us -> 21.1 us  [gather_columns(): lax.all_to_all(copies, axis_name, split_axis=0, concat_axis=0, tiled=True)]
    all_to_all x0 -> x2, waiting for transfers between devices: none -> 19.4 us  [all_by_exchange(): blocks = lax.all_to_all(blocks, axis, split_axis=0, concat_axis=0)]
    all_gather x2, blocking collectives: 37.5 us -> 53.2 us  [local(): lax.all_gather(part, 'req', axis=1, tiled=True)]
    all_to_all x3 -> x2, starting transfers between devices: 24.7 us -> 14.8 us  [gather_columns(): lax.all_to_all(copies, axis_name, split_axis=0, concat_axis=0, tiled=True)]
    all_to_all x0 -> x2, starting transfers between devices: none -> 8.24 us  [all_by_exchange(): blocks = lax.all_to_all(blocks, axis, split_axis=0, concat_axis=0)]
    all_to_all x1, blocking collectives: 20.2 us -> 14.8 us  [sum_scatter_columns(): lax.all_to_all(chunks, axis_name, split_axis=0, concat_axis=0, tiled=True)]
  transfers between devices with their start and end apart: 4 -> 5, of which waited for: 1 -> 4; matrix products, arithmetic and copies ran while one was open for 2% -> 3% of each run, Pallas kernels for 0% -> 0%
where the time goes in v1:
time: 257 us; the launch traced here: 256 us
  blocking collectives  141 us (55%)
  waiting for transfers between devices  53.3 us (21%)
  starting transfers between devices  28 us (11%)
  local copies, waits for them, and re-layouts  16.9 us (7%)
  other arithmetic  8.68 us (3%)
  matrix products  7.42 us (3%)
    all_to_all x2, blocking collectives, all_by_exchange(): blocks = lax.all_to_all(blocks, axis, split_axis=0, concat_axis=0)  58.3 us
    all_gather x2, blocking collectives, local(): lax.all_gather(part, 'req', axis=1, tiled=True)  53.2 us
    all_to_all x2, waiting for transfers between devices, gather_columns(): lax.all_to_all(copies, axis_name, split_axis=0, concat_axis=0, tiled=True)  21.1 us
    all_to_all x2, waiting for transfers between devices, all_by_exchange(): blocks = lax.all_to_all(blocks, axis, split_axis=0, concat_axis=0)  19.4 us
    all_to_all x1, blocking collectives, gather_columns(): lax.all_to_all(copies, axis_name, split_axis=0, concat_axis=0, tiled=True)  14.9 us
    all_to_all x2, starting transfers between devices, gather_columns(): lax.all_to_all(copies, axis_name, split_axis=0, concat_axis=0, tiled=True)  14.8 us
    all_to_all x1, blocking collectives, sum_scatter_columns(): lax.all_to_all(chunks, axis_name, split_axis=0, concat_axis=0, tiled=True)  14.8 us
    all_to_all x1, waiting for transfers between devices, local(): lax.all_to_all(outgoing, 'seq', split_axis=0, concat_axis=0, tiled=True)  12.8 us
  transfers between devices with their start and end apart: 5, of which 4 were waited for; matrix products, arithmetic and copies ran while one was open for 3% of the time, Pallas kernels for 0%

profile of v1, /device:TPU:8, one launch (start us, length us, event | category | flops | bytes accessed | tf_op | source)
XLA Modules:
  0.0 256.0 jit_solution(8086912626894675753)
XLA Ops:
  0.0 0.9 reshape.289
  0.9 1.0 multiply_reduce_fusion.2
  2.1 1.0 fusion.26
  3.1 0.8 broadcast_in_dim.66
  3.9 10.2 %all-to-all-start = ((f32[32,24,80]{2,1,0:T(8,128)}), f32[32,24,80]{2,1,0:T(8,128)S(1)}, u32[]{:S(2)}, u32[]{:S(2)}) async-start(f32[32,24,80]{2,1,0:T(8,128)} %broadcast_in_dim.66), calls=%async_computation | async-start | bytes 786432 | tf_op jit(solution)/shard_map/all_to_all | solution.py:54
  14.4 0.4 copy.66
  14.8 0.8 copy-done.4
  15.6 1.2 copy.67
  17.0 11.9 %all-to-all-done = f32[32,24,80]{2,1,0:T(8,128)S(1)} async-done(((f32[32,24,80]{2,1,0:T(8,128)}), f32[32,24,80]{2,1,0:T(8,128)S(1)}, u32[]{:S(2)}, u32[]{:S(2)}) %all-to-all-start) | async-done | bytes 245792 | tf_op jit(solution)/shard_map/all_to_all | solution.py:54
  29.5 0.4 copy-done.1
  30.1 0.5 fusion.47
  30.6 0.4 copy.70
  31.0 0.5 fusion.18
  31.5 0.4 copy.69
  32.1 0.6 convolution_bitcast_fusion
  33.4 0.9 pad_maximum_fusion
  34.3 4.9 %all-to-all-start.1 = ((f32[32,24,96]{2,1,0:T(8,128)}), f32[32,24,96]{2,1,0:T(8,128)S(1)}, u32[]{:S(2)}, u32[]{:S(2)}) async-start(f32[32,24,96]{2,1,0:T(8,128)} %pad_maximum_fusion), calls=%async_computation.1 | async-start | bytes 786432 | tf_op jit(solution)/shard_map/all_to_all | solution.py:142
  39.6 1.1 fusion.48
  40.9 12.8 %all-to-all-done.1 = f32[32,24,96]{2,1,0:T(8,128)S(1)} async-done(((f32[32,24,96]{2,1,0:T(8,128)}), f32[32,24,96]{2,1,0:T(8,128)S(1)}, u32[]{:S(2)}, u32[]{:S(2)}) %all-to-all-start.1) | async-done | bytes 294944 | tf_op jit(solution)/shard_map/all_to_all | solution.py:142
  54.2 0.3 fusion.16
  54.5 0.4 convolution_bitcast_fusion.1
  56.5 0.6 gather_fusion
  57.1 0.6 gather_fusion.1
  57.7 0.3 fusion.15
  58.2 0.9 reshape.332
  59.2 4.7 %all-to-all-start.2 = ((bf16[32,2,576]{2,1,0:T(2,128)(2,1)}), bf16[32,2,576]{2,1,0:T(2,128)(2,1)S(1)}, u32[]{:S(2)}, u32[]{:S(2)}) async-start(bf16[32,2,576]{2,1,0:T(2,128)(2,1)} %reshape.332), calls=%async_computation.2 | async-start | bytes 163840 | tf_op jit(solution)/shard_map/all_to_all | solution.py:54
  63.9 9.2 %all-to-all-done.2 = bf16[32,2,576]{2,1,0:T(2,128)(2,1)S(1)} async-done(((bf16[32,2,576]{2,1,0:T(2,128)(2,1)}), bf16[32,2,576]{2,1,0:T(2,128)(2,1)S(1)}, u32[]{:S(2)}, u32[]{:S(2)}) %all-to-all-start.2) | async-done | bytes 73760 | tf_op jit(solution)/shard_map/all_to_all | solution.py:54
  73.1 32.6 %all_to_all.45 = bf16[16,96,256]{2,1,0:T(8,128)(2,1)S(1)} all-to-all(bf16[16,96,256]{2,1,0:T(8,128)(2,1)S(1)} %stack.8), channel_id=1, replica_groups=mesh['seq'=32,'req'=16] {'req'}, dimensions={0} | all-to-all | bytes 1572864 | tf_op jit(solution)/shard_map/all_to_all | solution.py:26
  105.8 25.6 %all_to_all.46 = bf16[16,96,256]{2,1,0:T(8,128)(2,1)S(1)} all-to-all(bf16[16,96,256]{2,1,0:T(8,128)(2,1)S(1)} %stack.9), channel_id=1, replica_groups=mesh['seq'=32,'req'=16] {'req'}, dimensions={0} | all-to-all | bytes 1572864 | tf_op jit(solution)/shard_map/all_to_all | solution.py:26
  131.5 1.0 stack.10
  132.4 3.6 %all-to-all-start.6 = ((bf16[16,96,256]{2,1,0:T(8,128)(2,1)}), bf16[16,96,256]{2,1,0:T(8,128)(2,1)S(1)}, u32[]{:S(2)}, u32[]{:S(2)}) async-start(bf16[16,96,256]{2,1,0:T(8,128)(2,1)} %stack.10), calls=%async_computation.6 | async-start | bytes 1572864 | tf_op jit(solution)/shard_map/all_to_all | solution.py:26
  136.6 0.4 copy-done.10
  137.2 0.4 reshape.334
  137.5 19.4 %all-to-all-done.6 = bf16[16,96,256]{2,1,0:T(8,128)(2,1)S(1)} async-done(((bf16[16,96,256]{2,1,0:T(8,128)(2,1)}), bf16[16,96,256]{2,1,0:T(8,128)(2,1)S(1)}, u32[]{:S(2)}, u32[]{:S(2)}) %all-to-all-start.6) | async-done | bytes 786464 | tf_op jit(solution)/shard_map/all_to_all | solution.py:26
  156.9 14.9 %all_to_all.47 = f32[32,1,1152]{2,1,0:T(1,128)S(1)} all-to-all(f32[32,1,1152]{2,1,0:T(1,128)S(1)} %reshape.334), channel_id=1, replica_groups=mesh['seq'=32,'req'=16] {'seq'}, dimensions={0} | all-to-all | bytes 294912 | tf_op jit(solution)/shard_map/all_to_all | solution.py:54
  171.8 1.0 stack.11
  172.8 4.6 %all-to-all-start.7 = ((bf16[16,96,256]{2,1,0:T(8,128)(2,1)}), bf16[16,96,256]{2,1,0:T(8,128)(2,1)}, u32[]{:S(2)}, u32[]{:S(2)}) async-start(bf16[16,96,256]{2,1,0:T(8,128)(2,1)} %stack.11), calls=%async_computation.7 | async-start | bytes 1572864 | tf_op jit(solution)/shard_map/all_to_all | solution.py:26
  177.6 35.1 %all-gather = bf16[1,256,1536]{1,2,0:T(8,128)(2,1)} all-gather(bf16[1,256,96]{1,2,0:T(8,128)(2,1)S(1)} %get-tuple-element.20), channel_id=2, replica_groups=mesh['seq'=32,'req'=16] {'req'}, dimensions={2}, use_global_device_ids=true | all-gather | bytes 835584 | tf_op jit(solution)/shard_map/all_gather | solution.py:89
  212.8 18.1 %all-gather.1 = bf16[1,256,1536]{1,2,0:T(8,128)(2,1)} all-gather(bf16[1,256,96]{1,2,0:T(8,128)(2,1)S(1)} %get-tuple-element.21), channel_id=3, replica_groups=mesh['seq'=32,'req'=16] {'req'}, dimensions={2}, use_global_device_ids=true | all-gather | bytes 835584 | tf_op jit(solution)/shard_map/all_gather | solution.py:89
  230.8 0.5 broadcast.251
  231.3 1.0 reduce.5
  233.1 0.7 add.165
  234.0 3.1 %fusion = f32[24,1024]{1,0:T(8,128)S(1)} fusion(bf16[1536,256]{1,0:T(8,128)(2,1)} %bitcast.26, bf16[1536,256]{1,0:T(8,128)(2,1)S(1)} %bitcast.79, bf16[1536,256]{1,0:T(8,128)(2,1)S(1)} %bitcast.78, bf16[1536,256]{1,0:T(8,128)(2,1)S(1)} %bitcast.77, f32[24,1536]{1,0:T(8,128)} %add.165, f32[1536]{0:T(1024)S(1)} %copy-done.16, f32[24]{0:T(128)S(1)} %rsqrt.25), kind=kOutput, calls=%fused_computation.2 | convolution fusion | flops 88190976 | bytes 3397728 | tf_op jit(solution)/shard_map/dot_general | solution.py:179
  237.2 0.5 convolution_multiply_fusion
  238.1 0.4 reshape.336
  238.5 14.8 %all_to_all.48 = f32[32,1,1152]{2,1,0:T(1,128)S(1)} all-to-all(f32[32,1,1152]{2,1,0:T(1,128)S(1)} %reshape.336), channel_id=1, replica_groups=mesh['seq'=32,'req'=16] {'seq'}, dimensions={0} | all-to-all | bytes 294912 | tf_op jit(solution)/shard_map/all_to_all | solution.py:63
  253.3 1.0 reduce.6
  254.6 1.4 add_convert_fusion.2
  (111 shorter events, 7.7 us)
Async XLA Ops:
  0.0 2.0 copy-start
  2.0 12.0 %copy-start.15 = (s32[6]{0:T(128)S(1)}, s32[6]{0:T(128)}, u32[]{:S(2)}) copy-start(s32[6]{0:T(128)} %param.21) | copy-start | bytes 76
  2.0 12.1 %copy-start.14 = (s32[6,8]{1,0:T(8,128)S(1)}, s32[6,8]{1,0:T(8,128)}, u32[]{:S(2)}) copy-start(s32[6,8]{1,0:T(8,128)} %param.20) | copy-start | bytes 580
  2.1 12.4 %copy-start.3 = (bf16[6,128,512]{2,1,0:T(8,128)(2,1)S(1)}, bf16[6,128,512]{2,1,0:T(8,128)(2,1)}, u32[]{:S(2)}) copy-start(bf16[6,128,512]{2,1,0:T(8,128)(2,1)} %param.18) | copy-start | bytes 2359300
  3.9 25.1 %all-to-all-start = ((f32[32,24,80]{2,1,0:T(8,128)}), f32[32,24,80]{2,1,0:T(8,128)S(1)}, u32[]{:S(2)}, u32[]{:S(2)}) async-start(f32[32,24,80]{2,1,0:T(8,128)} %broadcast_in_dim.66), calls=%async_computation | async-start | bytes 786432 | tf_op jit(solution)/shard_map/all_to_all | solution.py:54
  14.4 1.1 copy-start.4
  29.2 0.7 copy-start.1
  30.6 1.5 copy-start.5
  33.4 5.8 %slice-start = ((f32[24,2560]{1,0:T(8,128)}), f32[24,512]{1,0:T(8,128)S(1)}, s32[]{:S(2)}) async-start(f32[24,2560]{1,0:T(8,128)} %copy-done.1), calls=%async_computation.9 | async-start | bytes 98304 | tf_op jit(solution)/shard_map/slice | solution.py:102
  34.3 5.1 %copy-start.2 = (f32[24,2560]{1,0:T(8,128)S(1)}, f32[24,2560]{1,0:T(8,128)}, u32[]{:S(2)}) copy-start(f32[24,2560]{1,0:T(8,128)} %copy-done.1) | copy-start | bytes 737284
  34.3 19.4 %all-to-all-start.1 = ((f32[32,24,96]{2,1,0:T(8,128)}), f32[32,24,96]{2,1,0:T(8,128)S(1)}, u32[]{:S(2)}, u32[]{:S(2)}) async-start(f32[32,24,96]{2,1,0:T(8,128)} %pad_maximum_fusion), calls=%async_computation.1 | async-start | bytes 786432 | tf_op jit(solution)/shard_map/all_to_all | solution.py:142
  57.7 6.1 %copy-start.9 = (bf16[1,96,1024]{2,1,0:T(8,128)(2,1)S(1)}, bf16[1,96,1024]{2,1,0:T(8,128)(2,1)}, u32[]{:S(2)}) copy-start(bf16[1,96,1024]{2,1,0:T(8,128)(2,1)} %param.24) | copy-start | bytes 589828
  59.2 13.9 %all-to-all-start.2 = ((bf16[32,2,576]{2,1,0:T(2,128)(2,1)}), bf16[32,2,576]{2,1,0:T(2,128)(2,1)S(1)}, u32[]{:S(2)}, u32[]{:S(2)}) async-start(bf16[32,2,576]{2,1,0:T(2,128)(2,1)} %reshape.332), calls=%async_computation.2 | async-start | bytes 163840 | tf_op jit(solution)/shard_map/all_to_all | solution.py:54
  132.4 24.5 %all-to-all-start.6 = ((bf16[16,96,256]{2,1,0:T(8,128)(2,1)}), bf16[16,96,256]{2,1,0:T(8,128)(2,1)S(1)}, u32[]{:S(2)}, u32[]{:S(2)}) async-start(bf16[16,96,256]{2,1,0:T(8,128)(2,1)} %stack.10), calls=%async_computation.6 | async-start | bytes 1572864 | tf_op jit(solution)/shard_map/all_to_all | solution.py:26
  136.0 0.9 copy-start.10
  172.8 4.6 %copy-start.12 = (f32[6,4,8]{2,1,0:T(4,128)S(1)}, f32[6,4,8]{2,1,0:T(4,128)}, u32[]{:S(2)}) copy-start(f32[6,4,8]{2,1,0:T(4,128)} %param.23) | copy-start | bytes 2308
  172.8 4.6 %copy-start.13 = (s32[6,4,8]{2,1,0:T(4,128)S(1)}, s32[6,4,8]{2,1,0:T(4,128)}, u32[]{:S(2)}) copy-start(s32[6,4,8]{2,1,0:T(4,128)} %param.22) | copy-start | bytes 2308
  172.8 4.8 %copy-start.11 = (bf16[1,512,96]{1,2,0:T(8,128)(2,1)S(1)}, bf16[1,512,96]{1,2,0:T(8,128)(2,1)}, u32[]{:S(2)}) copy-start(bf16[1,512,96]{1,2,0:T(8,128)(2,1)} %param.25) | copy-start | bytes 294916
  172.8 61.2 %all-to-all-start.7 = ((bf16[16,96,256]{2,1,0:T(8,128)(2,1)}), bf16[16,96,256]{2,1,0:T(8,128)(2,1)}, u32[]{:S(2)}, u32[]{:S(2)}) async-start(bf16[16,96,256]{2,1,0:T(8,128)(2,1)} %stack.11), calls=%async_computation.7 | async-start | bytes 1572864 | tf_op jit(solution)/shard_map/all_to_all | solution.py:26
  232.6 1.2 copy-start.8
  232.6 1.4 copy-start.16
  234.0 3.2 %copy-start.6 = (bf16[1,256,1536]{1,2,0:T(8,128)(2,1)S(1)}, bf16[1,256,1536]{1,2,0:T(8,128)(2,1)}, u32[]{:S(2)}) copy-start(bf16[1,256,1536]{1,2,0:T(8,128)(2,1)} %all-gather) | copy-start | bytes 2359300
  234.0 3.2 %copy-start.7 = (bf16[1,256,1536]{1,2,0:T(8,128)(2,1)S(1)}, bf16[1,256,1536]{1,2,0:T(8,128)(2,1)}, u32[]{:S(2)}) copy-start(bf16[1,256,1536]{1,2,0:T(8,128)(2,1)} %all-gather.1) | copy-start | bytes 2359300
